TPU v7x, 512 devices: a whole 4x8x8 slice. The times are simulated.
512 devices in a mesh: dp: 16 (over x, z_lo), blk: 32 (over y, z_hi, core).
Axes of the slice: x: 4, y: 8, z: 8 (z_hi: 2, z_lo: 4; z = z_hi * 4 + z_lo), core: 2. Of those that a mesh axis runs over, the one named last changes fastest.
Arguments:
- query_rows: bfloat16 [16, 4096, 1024], P('dp', 'blk'), may hold values from -160 to 160
- key_rows: bfloat16 [16, 4096, 1024], P('dp', 'blk'), may hold values from -6 to 6
- value_rows: bfloat16 [16, 4096, 1024], P('dp', 'blk'), may hold values from -6 to 6
- grad_out: bfloat16 [16, 4096, 1024], P('dp', 'blk'), may hold values from -6 to 6
- pos_keys: bfloat16 [512, 1024], P('blk'), may hold values from -3 to 3
- bias_content: float32 [1024], replicated, may hold values from -3 to 3
- bias_position: float32 [1024], replicated, may hold values from -3 to 3
Outputs:
- query_gradient: bfloat16 [16, 4096, 1024], P('dp', 'blk')
- grad_key: bfloat16 [16, 4096, 1024], P('dp', 'blk')
- grad_value: bfloat16 [16, 4096, 1024], P('dp', 'blk')
- grad_pos_keys: float32 [512, 1024], P('blk')
All inputs are finite; a program needn't handle non-finite values.
Results may differ from a plain program's by a relative error of at most 0.015.
The roundings to bfloat16 on the way count: a program that leaves them out, or rounds other values in their place, can miss the bound.
Values may be sent and summed in bfloat16 or wider, within the bound.
A program may use at most 64 MiB of HBM per device.

v0:
```python
import jax
import jax.numpy as jnp
from jax import lax
from jax.sharding import PartitionSpec as P

DH = 64


def passed_along(value, axis, steps):
    count = lax.axis_size(axis)
    pairs = [(source, (source + steps) % count) for source in range(count)]
    return lax.ppermute(value, axis, pairs)


def relative_select(products):
    heads_count, frames, spread = products.shape
    flipped = products[:, :, ::-1]
    flattened = flipped.reshape(heads_count, frames * spread)
    window = flattened[:, frames - 1 : frames - 1 + frames * (spread - 1)]
    return window.reshape(heads_count, frames, spread - 1)[:, :, :frames]


def relative_place(gradient):
    heads_count, frames = (gradient.shape[0], gradient.shape[1])
    spread = 2 * frames
    padded = jnp.pad(gradient, ((0, 0), (0, 0), (0, spread - 1 - frames)))
    flattened = padded.reshape(heads_count, frames * (spread - 1))
    flattened = jnp.pad(flattened, ((0, 0), (frames - 1, 1)))
    return flattened.reshape(heads_count, frames, spread)[:, :, ::-1]


def group_grads(
    content_in, position_in, keys_all, values_all, grad_rows, band_own, band_prev, head_dim
):
    factor = head_dim ** (-0.5)
    frames = content_in.shape[0]

    def split_heads(matrix):
        return matrix.reshape(matrix.shape[0], -1, head_dim)

    def join_head_axes(matrix):
        return matrix.reshape(matrix.shape[0], -1)

    content_h = split_heads(content_in)
    position_per_head = split_heads(position_in)
    keys_h = split_heads(keys_all)
    values_h = split_heads(values_all)
    grad_h = split_heads(grad_rows)
    current_band_per_head = split_heads(band_own)
    earlier_band_per_head = split_heads(band_prev)
    content = jnp.einsum("ihd,jhd->hij", content_h, keys_h, preferred_element_type=jnp.float32)
    current_position = relative_select(
        jnp.einsum(
            "fju,tju->jft",
            position_per_head,
            current_band_per_head,
            preferred_element_type=jnp.float32,
        )
    )
    earlier_position = relative_select(
        jnp.einsum(
            "fju,tju->jft",
            position_per_head,
            earlier_band_per_head,
            preferred_element_type=jnp.float32,
        )
    )
    scores = (content + jnp.concatenate([current_position, earlier_position], axis=2)) * factor
    row_max = jnp.max(scores, axis=2, keepdims=True)
    shifted = jnp.exp(scores - row_max)
    attention = shifted / jnp.sum(shifted, axis=2, keepdims=True)
    attention_b = attention.astype(jnp.bfloat16)
    grad_weights = jnp.einsum("ihd,jhd->hij", grad_h, values_h, preferred_element_type=jnp.float32)
    row_delta = jnp.sum(attention * grad_weights, axis=2, keepdims=True)
    dscore = (attention * (grad_weights - row_delta) * factor).astype(jnp.bfloat16)
    current_location = relative_place(dscore[:, :, :frames])
    earlier_location = relative_place(dscore[:, :, frames:])
    query_gradient = jnp.einsum("hij,jhd->ihd", dscore, keys_h, preferred_element_type=jnp.float32)
    query_gradient = query_gradient + jnp.einsum(
        "urk,kuo->ruo", current_location, current_band_per_head, preferred_element_type=jnp.float32
    )
    query_gradient = query_gradient + jnp.einsum(
        "urk,kuo->ruo", earlier_location, earlier_band_per_head, preferred_element_type=jnp.float32
    )
    grad_keys = jnp.einsum("hij,ihd->jhd", dscore, content_h, preferred_element_type=jnp.float32)
    grad_values = jnp.einsum(
        "hij,ihd->jhd", attention_b, grad_h, preferred_element_type=jnp.float32
    )
    current_gradient = jnp.einsum(
        "zfg,fzw->gzw", current_location, position_per_head, preferred_element_type=jnp.float32
    )
    prev_grad = jnp.einsum(
        "zfg,fzw->gzw", earlier_location, position_per_head, preferred_element_type=jnp.float32
    )
    return (
        join_head_axes(query_gradient),
        join_head_axes(grad_keys),
        join_head_axes(grad_values),
        join_head_axes(current_gradient),
        join_head_axes(prev_grad),
    )


def local(query_rows, key_rows, value_rows, grad_out, pos_keys, bias_content, bias_position):
    band_table = lax.all_gather(pos_keys, "blk", axis=0, tiled=True)
    prev_key, prev_value = passed_along((key_rows, value_rows), "blk", 1)
    frames = query_rows.shape[1]
    model_width = query_rows.shape[2]
    band_rows = band_table.shape[0] // 2
    group_width = min(model_width, max(DH, 256 // DH * DH))
    group_count = model_width // group_width

    def to_groups(matrix):
        return matrix.reshape(matrix.shape[0], group_count, group_width).transpose(1, 0, 2)

    def from_groups(matrix):
        return matrix.transpose(1, 0, 2).reshape(matrix.shape[1], model_width)

    own_band = to_groups(band_table[:band_rows])
    prev_band = to_groups(band_table[band_rows:])
    query_content = (query_rows.astype(jnp.float32) + bias_content).astype(jnp.bfloat16)
    query_position = (query_rows.astype(jnp.float32) + bias_position).astype(jnp.bfloat16)

    def one_group(packed):
        return group_grads(*packed, DH)

    def one_recording(band_sums, inputs):
        content_in, position_in, own_keys, own_values, prev_keys, prev_values, grad_rows = inputs
        keys_all = jnp.concatenate([own_keys, prev_keys], axis=0)
        values_all = jnp.concatenate([own_values, prev_values], axis=0)
        group_out = lax.map(
            one_group,
            (
                to_groups(content_in),
                to_groups(position_in),
                to_groups(keys_all),
                to_groups(values_all),
                to_groups(grad_rows),
                own_band,
                prev_band,
            ),
        )
        query_gradient = from_groups(group_out[0])
        grad_keys = from_groups(group_out[1])
        grad_values = from_groups(group_out[2])
        new_sums = (
            band_sums[0] + from_groups(group_out[3]),
            band_sums[1] + from_groups(group_out[4]),
        )
        return (
            new_sums,
            (
                query_gradient.astype(jnp.bfloat16),
                grad_keys[:frames],
                grad_keys[frames:].astype(jnp.bfloat16),
                grad_values[:frames],
                grad_values[frames:].astype(jnp.bfloat16),
            ),
        )

    initial = (
        jnp.zeros((band_rows, model_width), jnp.float32),
        jnp.zeros((band_rows, model_width), jnp.float32),
    )
    band_sums, stacked = lax.scan(
        one_recording,
        initial,
        (query_content, query_position, key_rows, value_rows, prev_key, prev_value, grad_out),
    )
    key_back, value_back = passed_along((stacked[2], stacked[4]), "blk", -1)
    grad_key = (stacked[1] + key_back.astype(jnp.float32)).astype(jnp.bfloat16)
    grad_value = (stacked[3] + value_back.astype(jnp.float32)).astype(jnp.bfloat16)
    band_terms = jnp.concatenate([band_sums[0], band_sums[1]], axis=0)
    summed = lax.psum(band_terms, ("dp", "blk"))
    owned_rows = band_terms.shape[0] // lax.axis_size("blk")
    grad_pos = lax.dynamic_slice_in_dim(summed, lax.axis_index("blk") * owned_rows, owned_rows, 0)
    return (stacked[0], grad_key, grad_value, grad_pos)


def solution(mesh):
    placed = (
        P("dp", "blk", None),
        P("dp", "blk", None),
        P("dp", "blk", None),
        P("dp", "blk", None),
        P("blk", None),
        P(),
        P(),
    )
    return jax.shard_map(
        local,
        mesh=mesh,
        in_specs=placed,
        out_specs=(
            P("dp", "blk", None),
            P("dp", "blk", None),
            P("dp", "blk", None),
            P("blk", None),
        ),
        check_vma=False,
    )
```

profile of v0, /device:TPU:1, one launch (start us, length us, event | category | flops | bytes accessed | tf_op | source)
XLA Modules:
  0.0 489.5 jit_solution(13562615246416783814)
XLA Ops:
  8.0 12.0 %collective-permute-start = (bf16[1,128,1024]{2,1,0:T(8,128)(2,1)}, bf16[1,128,1024]{2,1,0:T(8,128)(2,1)S(1)}, u32[]{:S(2)}, u32[]{:S(2)}) collective-permute-start(bf16[1,128,1024]{2,1,0:T(8,128)(2,1)} %param.10), channel_id=1, source_target_pairs={{0,1},{1,2},{2,3},{3,4},{4,5},{5,6},{6,7},{7,8},{8,9},{9,10},{10,1... | collective-permute-start | bytes 786440 | tf_op jit(solution)/shard_map/ppermute | solution.py:12
  20.0 1.9 collective-permute-start.1
  22.0 1.1 copy.27
  23.1 1.1 copy.34
  24.2 1.1 fusion.28
  25.5 0.8 copy.30
  26.3 0.8 copy.33
  27.3 4.3 collective-permute-done.1
  31.8 0.9 maximum_bitcast_fusion
  32.8 73.3 %all-gather.2.cloned.1.call-done = bf16[512,1024]{1,0:T(8,128)(2,1)} async-done(((bf16[16,1024]{1,0:T(8,128)(2,1)}), bf16[512,1024]{1,0:T(8,128)(2,1)}) %all-gather.2.cloned.1.call-update) | async-done | bytes 1048592 | tf_op jit(solution)/shard_map/all_gather | solution.py:105
  106.1 1.3 fusion.30
  107.6 1.0 copy.32
  108.6 88.7 %while.37 = (s32[]{:T(128)}, bf16[4,128,256]{1,2,0:T(8,128)(2,1)S(1)}, f32[4,256,256]{1,2,0:T(8,128)}, f32[4,256,256]{1,2,0:T(8,128)}, f32[4,256,256]{1,2,0:T(8,...) while((s32[]{:T(128)}, ...), condition=%wide.region_4.5_spmd, body=%wide.region_0.4_spmd.sunk | while | flops 239307520 | bytes 39503472 | solution.py:131
  108.6 1.1 constant_dynamic-slice_fusion.15
  109.6 0.9 constant_dynamic-slice_fusion.16
  110.8 0.9 constant_dynamic-slice_fusion.19
  111.7 0.9 constant_dynamic-slice_fusion.20
  117.8 2.5 fusion.135
  120.3 1.2 fusion.136
  122.4 0.8 rev.30
  124.4 0.8 rev.31
  126.1 2.6 fusion.138
  130.7 1.1 constant_dynamic-slice_fusion.15
  131.8 0.9 constant_dynamic-slice_fusion.16
  133.0 0.9 constant_dynamic-slice_fusion.19
  133.8 0.9 constant_dynamic-slice_fusion.20
  140.0 2.5 fusion.135
  142.5 1.2 fusion.136
  144.6 0.8 rev.30
  146.6 0.8 rev.31
  148.2 2.6 fusion.138
  150.8 0.8 constant_dynamic-update-slice_fusion.9
  152.9 1.1 constant_dynamic-slice_fusion.15
  154.0 0.9 constant_dynamic-slice_fusion.16
  155.2 0.9 constant_dynamic-slice_fusion.19
  156.0 0.9 constant_dynamic-slice_fusion.20
  162.1 2.5 fusion.135
  164.7 1.2 fusion.136
  166.7 0.8 rev.30
  170.4 2.6 fusion.138
  173.0 0.8 constant_dynamic-update-slice_fusion.9
  174.2 0.8 constant_dynamic-update-slice_fusion.10
  175.1 1.1 constant_dynamic-slice_fusion.15
  176.2 0.9 constant_dynamic-slice_fusion.16
  177.3 0.9 constant_dynamic-slice_fusion.19
  178.2 0.9 constant_dynamic-slice_fusion.20
  184.3 2.5 fusion.135
  186.8 1.2 fusion.136
  192.6 2.6 fusion.138
  196.4 0.8 constant_dynamic-update-slice_fusion.10
  197.2 1.7 copy.49
  199.3 1.5 pad_maximum_fusion
  200.8 1.2 copy-done.7
  202.0 0.8 copy.45
  202.9 2.2 collective-permute-start.2
  205.1 0.9 copy.47
  206.0 1.9 collective-permute-start.3
  208.0 0.8 copy.43
  209.2 8.3 %collective-permute-done.2 = bf16[1,128,1024]{2,1,0:T(8,128)(2,1)} collective-permute-done((bf16[1,128,1024]{2,1,0:T(8,128)(2,1)}, bf16[1,128,1024]{2,1,0:T(8,128)(2,1)}, u32[]{:S(2)}, u32[]{:S(2)}) %collective-permute-start.2) | collective-permute-done | bytes 262176 | tf_op jit(solution)/shard_map/ppermute | solution.py:12
  217.5 1.7 add_convert_fusion.1
  219.2 4.7 collective-permute-done.3
  223.9 1.7 add_convert_fusion
  225.6 255.6 %all-reduce.5.cloned.1.call-done = f32[512,1024]{1,0:T(8,128)} async-done(((f32[512,1024]{1,0:T(8,128)}), f32[512,1024]{1,0:T(8,128)}) %all-reduce.5.cloned.1.call-update) | async-done | bytes 2097168 | tf_op jit(solution)/shard_map/psum | solution.py:174
  481.2 1.5 constant_dynamic-slice_fusion.7
  (217 shorter events, 42.5 us)
Async XLA Ops:
  7.2 19.1 %copy-start.9 = (bf16[1,128,1024]{2,1,0:T(8,128)(2,1)S(1)}, bf16[1,128,1024]{2,1,0:T(8,128)(2,1)}, u32[]{:S(2)}) copy-start(bf16[1,128,1024]{2,1,0:T(8,128)(2,1)} %param.12) | copy-start | bytes 786436
  7.2 98.9 %all-gather.2.cloned.1.call-start = ((), (), s32[]{:S(2)}) async-start(), calls=%async_computation | async-start | bytes 1081344 | tf_op jit(solution)/shard_map/all_gather | solution.py:105
  7.9 473.3 %all-reduce.5.cloned.1.call-start = ((), (), s32[]{:S(2)}) async-start(), calls=%async_computation.1 | async-start | bytes 4194304 | tf_op jit(solution)/shard_map/psum | solution.py:174
  8.0 19.2 %collective-permute-start = (bf16[1,128,1024]{2,1,0:T(8,128)(2,1)}, bf16[1,128,1024]{2,1,0:T(8,128)(2,1)S(1)}, u32[]{:S(2)}, u32[]{:S(2)}) collective-permute-start(bf16[1,128,1024]{2,1,0:T(8,128)(2,1)} %param.10), channel_id=1, source_target_pairs={{0,1},{1,2},{2,3},{3,4},{4,5},{5,6},{6,7},{7,8},{8,9},{9,10},{10,1... | collective-permute-start | bytes 786440 | tf_op jit(solution)/shard_map/ppermute | solution.py:12
  20.0 11.7 %collective-permute-start.1 = (bf16[1,128,1024]{2,1,0:T(8,128)(2,1)}, bf16[1,128,1024]{2,1,0:T(8,128)(2,1)S(1)}, u32[]{:S(2)}, u32[]{:S(2)}) collective-permute-start(bf16[1,128,1024]{2,1,0:T(8,128)(2,1)} %param.11), channel_id=1, source_target_pairs={{0,1},{1,2},{2,3},{3,4},{4,5},{5,6},{6,7},{7,8},{8,9},{9,10},{10,1... | collective-permute-start | bytes 786440 | tf_op jit(solution)/shard_map/ppermute | solution.py:12
  32.8 75.8 %copy-start.12 = (pred[255]{0:T(512)(128)(4,1)S(1)}, pred[255]{0:T(512)(128)(4,1)}, u32[]{:S(2)}) copy-start(pred[255]{0:T(512)(128)(4,1)} %constant.83.clone.1) | copy-start | bytes 769
  108.6 1.9 copy-start.2
  108.6 5.4 %copy-start.4 = (bf16[4,128,256]{1,2,0:T(8,128)(2,1)}, bf16[4,128,256]{1,2,0:T(8,128)(2,1)S(1)}, u32[]{:S(2)}) copy-start(bf16[4,128,256]{1,2,0:T(8,128)(2,1)S(1)} %get-tuple-element.393) | copy-start | bytes 786436 | tf_op jit(solution)/shard_map/while/body/eval_jaxpr/while
  108.6 6.4 %copy-start = (bf16[4,256,256]{1,2,0:T(8,128)(2,1)}, bf16[4,256,256]{1,2,0:T(8,128)(2,1)S(1)}, u32[]{:S(2)}) copy-start(bf16[4,256,256]{1,2,0:T(8,128)(2,1)S(1)} %get-tuple-element.395) | copy-start | bytes 1572868 | tf_op jit(solution)/shard_map/while/body/eval_jaxpr/while
  128.6 2.0 copy-start.1
  128.6 2.0 copy-start.3
  128.7 2.0 copy-start.5
  130.7 2.0 copy-start.2
  130.7 5.4 %copy-start.4 = (bf16[4,128,256]{1,2,0:T(8,128)(2,1)}, bf16[4,128,256]{1,2,0:T(8,128)(2,1)S(1)}, u32[]{:S(2)}) copy-start(bf16[4,128,256]{1,2,0:T(8,128)(2,1)S(1)} %get-tuple-element.393) | copy-start | bytes 786436 | tf_op jit(solution)/shard_map/while/body/eval_jaxpr/while
  130.7 6.4 %copy-start = (bf16[4,256,256]{1,2,0:T(8,128)(2,1)}, bf16[4,256,256]{1,2,0:T(8,128)(2,1)S(1)}, u32[]{:S(2)}) copy-start(bf16[4,256,256]{1,2,0:T(8,128)(2,1)S(1)} %get-tuple-element.395) | copy-start | bytes 1572868 | tf_op jit(solution)/shard_map/while/body/eval_jaxpr/while
  150.8 2.1 copy-start.1
  150.8 2.1 copy-start.3
  150.8 2.1 copy-start.5
  152.9 2.0 copy-start.2
  152.9 5.4 %copy-start.4 = (bf16[4,128,256]{1,2,0:T(8,128)(2,1)}, bf16[4,128,256]{1,2,0:T(8,128)(2,1)S(1)}, u32[]{:S(2)}) copy-start(bf16[4,128,256]{1,2,0:T(8,128)(2,1)S(1)} %get-tuple-element.393) | copy-start | bytes 786436 | tf_op jit(solution)/shard_map/while/body/eval_jaxpr/while
  152.9 6.4 %copy-start = (bf16[4,256,256]{1,2,0:T(8,128)(2,1)}, bf16[4,256,256]{1,2,0:T(8,128)(2,1)S(1)}, u32[]{:S(2)}) copy-start(bf16[4,256,256]{1,2,0:T(8,128)(2,1)S(1)} %get-tuple-element.395) | copy-start | bytes 1572868 | tf_op jit(solution)/shard_map/while/body/eval_jaxpr/while
  173.0 2.1 copy-start.1
  173.0 2.1 copy-start.3
  173.0 2.1 copy-start.5
  175.1 2.0 copy-start.2
  175.1 5.4 %copy-start.4 = (bf16[4,128,256]{1,2,0:T(8,128)(2,1)}, bf16[4,128,256]{1,2,0:T(8,128)(2,1)S(1)}, u32[]{:S(2)}) copy-start(bf16[4,128,256]{1,2,0:T(8,128)(2,1)S(1)} %get-tuple-element.393) | copy-start | bytes 786436 | tf_op jit(solution)/shard_map/while/body/eval_jaxpr/while
  175.1 6.4 %copy-start = (bf16[4,256,256]{1,2,0:T(8,128)(2,1)}, bf16[4,256,256]{1,2,0:T(8,128)(2,1)S(1)}, u32[]{:S(2)}) copy-start(bf16[4,256,256]{1,2,0:T(8,128)(2,1)S(1)} %get-tuple-element.395) | copy-start | bytes 1572868 | tf_op jit(solution)/shard_map/while/body/eval_jaxpr/while
  195.2 2.0 copy-start.1
  195.2 2.0 copy-start.3
  195.2 2.0 copy-start.5
  197.2 1.7 copy-start.10
  197.2 1.7 copy-start.6
  200.7 1.2 copy-start.7
  200.7 4.3 copy-start.8
  202.0 6.0 %copy-start.11 = (bf16[4,128,256]{1,2,0:T(8,128)(2,1)S(1)}, bf16[4,128,256]{1,2,0:T(8,128)(2,1)}, u32[]{:S(2)}) copy-start(bf16[4,128,256]{1,2,0:T(8,128)(2,1)} %copy-done.10) | copy-start | bytes 786436
  202.9 14.6 %collective-permute-start.2 = (bf16[1,128,1024]{2,1,0:T(8,128)(2,1)}, bf16[1,128,1024]{2,1,0:T(8,128)(2,1)}, u32[]{:S(2)}, u32[]{:S(2)}) collective-permute-start(bf16[1,128,1024]{2,1,0:T(8,128)(2,1)} %copy.45), channel_id=1, source_target_pairs={{0,31},{1,0},{2,1},{3,2},{4,3},{5,4},{6,5},{7,6},{8,7},{9,8},{10,9... | collective-permute-start | bytes 786440 | tf_op jit(solution)/shard_map/ppermute | solution.py:12
  206.0 17.9 %collective-permute-start.3 = (bf16[1,128,1024]{2,1,0:T(8,128)(2,1)}, bf16[1,128,1024]{2,1,0:T(8,128)(2,1)}, u32[]{:S(2)}, u32[]{:S(2)}) collective-permute-start(bf16[1,128,1024]{2,1,0:T(8,128)(2,1)} %copy.47), channel_id=1, source_target_pairs={{0,31},{1,0},{2,1},{3,2},{4,3},{5,4},{6,5},{7,6},{8,7},{9,8},{10,9... | collective-permute-start | bytes 786440 | tf_op jit(solution)/shard_map/ppermute | solution.py:12
Sparse Core Ops, SparseCore 0:
  11.3 94.7 all-gather.1
  200.9 280.2 all-reduce.4
where the time goes:
time: 491 us; the launch traced here: 489 us
  waiting for transfers between devices  347 us (71%)
  local copies, waits for them, and re-layouts  66.6 us (14%)
  matrix products  35.4 us (7%)
  starting transfers between devices  18.1 us (4%)
  between operations  14.3 us (3%)
  other arithmetic  7 us (1%)
    psum x1, waiting for transfers between devices, local(): summed = lax.psum(band_terms, ('dp', 'blk'))  256 us
    all_gather x1, waiting for transfers between devices, local(): band_table = lax.all_gather(pos_keys, 'blk', axis=0, tiled=True)  73.3 us
    ppermute x4, starting transfers between devices, passed_along(): return lax.ppermute(value, axis, pairs)  18 us
    ppermute x4, waiting for transfers between devices, passed_along(): return lax.ppermute(value, axis, pairs)  17.3 us
    dynamic_slice x28, local copies, waits for them, and re-layouts, one_recording(): lax.map(one_group, (to_groups(content_in), to_groups(position_in), to_gro...  14.9 us
    dot_general x4, matrix products, group_grads(): jnp.einsum('hij,ihd->jhd', dscore, content_h, preferred_element_type=jnp....  10.3 us
    dot_general x4, matrix products, group_grads(): jnp.einsum('hij,jhd->ihd', dscore, keys_h, preferred_element_type=jnp.flo...  10.1 us
  transfers between devices with their start and end apart: 6, of which 5 were waited for; matrix products, arithmetic and copies ran while one was open for 3% of the time, Pallas kernels for 0%

commit v1 on v0

v1 whole, which is shorter than its diff:
```python
import functools

import jax
import jax.numpy as jnp
from jax import lax
from jax.experimental import pallas as pl
from jax.experimental.pallas import tpu as pltpu
from jax.sharding import PartitionSpec as P

MESH = pl.DeviceIdType.MESH
DH = 64
LANES = 2 * DH
FRAMES = 128
F32, BF16 = jnp.float32, jnp.bfloat16
NX, NY, NZ, ZL = 4, 8, 8, 4
QUERY, GRAD, KEY, VALUE = range(4)


def contract_lanes(a, b):
    return lax.dot_general(a, b, (((1,), (1,)), ((), ())), preferred_element_type=F32)


def contract_rows(a, b):
    return lax.dot_general(a, b, (((0,), (0,)), ((), ())), preferred_element_type=F32)


def place_roll(x):
    rows = x.shape[0]
    blocks = [
        pltpu.roll(x[8 * a : 8 * a + 8], (127 - 8 * a) % 128, 1) for a in range(rows // 8)
    ]
    x = jnp.concatenate(blocks, axis=0)
    row = lax.broadcasted_iota(jnp.int32, x.shape, 0)
    for bit in range(3):
        moved = pltpu.roll(x, 128 - 2**bit, 1)
        x = jnp.where(((row >> bit) & 1) == 1, moved, x)
    return x


def pair_grads(q, grad, keys, values, table, bias_c, bias_p):
    first = lax.broadcasted_iota(jnp.int32, (FRAMES, LANES), 1) < DH

    def stacked(x):
        zero = jnp.zeros_like(x)
        both = jnp.concatenate([jnp.where(first, x, zero), jnp.where(first, zero, x)], axis=0)
        return both.astype(BF16)

    q32 = q.astype(F32)
    content_in = stacked(q32 + bias_c)
    position_in = stacked(q32 + bias_p)
    grad_in = stacked(grad.astype(F32))
    content = contract_lanes(content_in, keys)
    spread = contract_lanes(position_in, table)
    weights = contract_lanes(grad_in, values)
    shape = (2 * FRAMES, FRAMES)
    frame = lax.broadcasted_iota(jnp.int32, shape, 0) & (FRAMES - 1)
    upper = lax.broadcasted_iota(jnp.int32, shape, 1) + frame >= FRAMES - 1

    def select(at):
        picked = jnp.where(upper, spread[:, at : at + 128], spread[:, at + 128 : at + 256])
        return pltpu.roll(picked, 1, 1, stride=1, stride_axis=0)

    factor = DH**-0.5
    s0 = (content[:, :128] + select(256)) * factor
    s1 = (content[:, 128:] + select(0)) * factor
    top = jnp.max(jnp.maximum(s0, s1), axis=1, keepdims=True)
    e0, e1 = jnp.exp(s0 - top), jnp.exp(s1 - top)
    inverse = 1.0 / jnp.sum(e0 + e1, axis=1, keepdims=True)
    a0, a1 = e0 * inverse, e1 * inverse
    w0, w1 = weights[:, :128], weights[:, 128:]
    delta = jnp.sum(a0 * w0 + a1 * w1, axis=1, keepdims=True)
    d0 = a0 * (w0 - delta) * factor
    d1 = a1 * (w1 - delta) * factor
    dscore = jnp.concatenate([d0, d1], axis=1).astype(BF16)
    attention = jnp.concatenate([a0, a1], axis=1).astype(BF16)
    p0, p1 = place_roll(d0), place_roll(d1)
    zero = jnp.zeros_like(p0)
    location = jnp.concatenate(
        [
            jnp.where(upper, p1, zero),
            jnp.where(upper, zero, p1),
            jnp.where(upper, p0, zero),
            jnp.where(upper, zero, p0),
        ],
        axis=1,
    ).astype(BF16)
    both = jnp.dot(
        jnp.concatenate([dscore, location], axis=1),
        jnp.concatenate([keys, table], axis=0),
        preferred_element_type=F32,
    )
    query_gradient = jnp.where(first, both[:FRAMES], both[FRAMES:])
    key_term = contract_rows(dscore, content_in)
    value_term = contract_rows(attention, grad_in)
    band_term = contract_rows(location, position_in)
    return query_gradient, key_term, value_term, band_term


def kernel(
    pairs,
    q_ref, k_ref, v_ref, g_ref, pos_ref, bc_ref, bp_ref,
    dq_ref, dk_ref, dv_ref, dp_ref,
    inp, kvp, tab, dqv, dkv0, dkv1, dkv1r, dkvo, band, band16, corer, ysend, yr, xsum, xsend, xr, zsend, zr, xg,
    in_sem, kv_s, kv_r, z_s, z_r, y_s, y_r, c_s, c_r, b_s, b_r, bc_s, bc_r, by_s, by_r, bx_s, bx_r, bz_s, bz_r,
    xg_s, xg_r, out_sem,
):
    groups = pairs // 2
    dp, blk = lax.axis_index("dp"), lax.axis_index("blk")
    x, zl = dp // ZL, dp % ZL
    y, zh, c = blk // 4, (blk // 2) % 2, blk % 2
    z = zh * ZL + zl
    count = 4 * NY

    def at(x_, y_, z_, c_):
        return (x_ * ZL + z_ % ZL, (y_ * 2 + z_ // ZL) * 2 + c_)

    following, before = (dp, (blk + 1) % count), (dp, (blk + count - 1) % count)
    partner = at(x, y, z, 1 - c)
    opposite = (dp, (y * 2 + 1 - zh) * 2 + c)
    y_peers = [at(x, (y + d) % NY, z, c) for d in range(1, NY)]
    x_peers = [at((x + d) % NX, y, z, c) for d in range(1, NX)]
    z_peers = [at(x, y, (z + d) % NZ, c) for d in range(1, NZ)]

    def remote(src, dst, send, recv, device):
        return pltpu.make_async_remote_copy(
            src_ref=src, dst_ref=dst, send_sem=send, recv_sem=recv, device_id=device, device_id_type=MESH
        )

    def wait_bytes(ref, sem):
        pltpu.make_async_copy(ref, ref, sem).wait()

    def cols(p):
        return pl.ds(p * LANES, LANES)

    barrier = pltpu.get_barrier_semaphore()
    peers = [following, before] + y_peers + x_peers + z_peers
    for peer in peers:
        pl.semaphore_signal(barrier, inc=1, device_id=peer, device_id_type=MESH)
    for p in range(pairs):
        for n, ref in ((QUERY, q_ref), (GRAD, g_ref), (KEY, k_ref), (VALUE, v_ref)):
            pltpu.make_async_copy(ref.at[0, :, cols(p)], inp.at[p, n], in_sem.at[p]).start()

    flip = (
        lax.broadcasted_iota(jnp.int32, (16, 16), 0) + lax.broadcasted_iota(jnp.int32, (16, 16), 1) == 15
    )
    turned = jnp.dot(
        jnp.where(flip, 1.0, 0.0).astype(BF16), pos_ref[...], preferred_element_type=F32
    ).astype(BF16)
    sy, sz, sc = NY - 1 - y, 1 - zh, 1 - c
    for p in range(pairs):
        tab[p, sy, sz, sc] = turned[:, p * LANES : (p + 1) * LANES]
    pl.semaphore_wait(barrier, len(peers))

    def shard(g, z_):
        return tab.at[pl.ds(2 * g, 2), sy, z_, sc]

    for g in range(groups):
        remote(shard(g, sz), shard(g, sz), z_s, z_r.at[g], opposite).start()
        for peer in y_peers:
            remote(shard(g, sz), shard(g, sz), y_s, y_r.at[g], peer).start()
        for p in (2 * g, 2 * g + 1):
            for n, ref in ((0, k_ref), (1, v_ref)):
                remote(ref.at[0, :, cols(p)], kvp.at[p, n], kv_s, kv_r.at[p], following).start()
    for g in range(groups):
        wait_bytes(shard(g, 1 - sz), z_r.at[g])
        for peer in y_peers:
            remote(shard(g, 1 - sz), shard(g, 1 - sz), y_s, y_r.at[g], peer).start()

    def share_table(g):
        wait_bytes(tab.at[pl.ds(2 * g, 2), pl.ds(0, NY - 1), :, 0], y_r.at[g])
        mine = tab.at[pl.ds(2 * g, 2), :, :, sc]
        remote(mine, mine, c_s, c_r.at[g], partner).start()

    def pair_step(p):
        wait_bytes(inp.at[p], in_sem.at[p])
        wait_bytes(kvp.at[p], kv_r.at[p])
        keys = jnp.concatenate([inp[p, KEY], kvp[p, 0]], axis=0)
        values = jnp.concatenate([inp[p, VALUE], kvp[p, 1]], axis=0)
        table = tab[p].reshape(32 * 16, LANES)
        lanes = slice(p * LANES, (p + 1) * LANES)
        dq, dk, dv, db = pair_grads(
            inp[p, QUERY], inp[p, GRAD], keys, values, table, bc_ref[:, lanes], bp_ref[:, lanes]
        )
        dqv[p] = dq.astype(BF16)
        pltpu.make_async_copy(dqv.at[p], dq_ref.at[0, :, cols(p)], out_sem).start()
        dkv0[p, 0] = dk[:FRAMES]
        dkv0[p, 1] = dv[:FRAMES]
        dkv1[p, 0] = dk[FRAMES:].astype(BF16)
        dkv1[p, 1] = dv[FRAMES:].astype(BF16)
        db = db.reshape(NY, 2, 2, 16, LANES)
        band[p] = db
        band16[p] = db.astype(BF16)

    def send_back(g):
        two = pl.ds(2 * g, 2)
        remote(band16.at[two, :, :, c], corer.at[two], bc_s, bc_r.at[g], partner).start()
        for p in (2 * g, 2 * g + 1):
            remote(dkv1.at[p], dkv1r.at[p], b_s, b_r.at[p], before).start()

    def chip_sum(g):
        two = pl.ds(2 * g, 2)
        wait_bytes(corer.at[two], bc_r.at[g])
        for p in (2 * g, 2 * g + 1):
            total = band[p, :, :, sc] + corer[p].astype(F32)
            ysend[p] = total.astype(BF16)
        for d, peer in enumerate(y_peers):
            sink = NY - 1 - (y + d + 1) % NY
            remote(ysend.at[two, sink], yr.at[d, two], by_s, by_r.at[g], peer).start()

    def y_sum(g):
        two = pl.ds(2 * g, 2)
        wait_bytes(yr.at[:, two], by_r.at[g])
        for p in (2 * g, 2 * g + 1):
            total = band[p, sy, :, sc] + corer[p, sy].astype(F32)
            for d in range(NY - 1):
                total = total + yr[d, p].astype(F32)
            xsum[p] = total
            xsend[p] = total.astype(BF16)

        @pl.when(x != g)
        def _():
            slot = (x + NX - g) % NX - 1
            remote(xsend.at[two], xr.at[slot], bx_s.at[g], bx_r, at(g, y, z, c)).start()

    share_table(0)
    for g in range(groups):
        wait_bytes(tab.at[pl.ds(2 * g, 2), :, :, 0], c_r.at[g])
        pair_step(2 * g)
        if g + 1 < groups:
            share_table(g + 1)
        pair_step(2 * g + 1)
        send_back(g)
        if g >= 1:
            chip_sum(g - 1)
        if g >= 2:
            y_sum(g - 2)
    chip_sum(groups - 1)
    y_sum(groups - 2)

    def finish_keys(p):
        wait_bytes(dkv1r.at[p], b_r.at[p])
        dkvo[p] = (dkv0[p] + dkv1r[p].astype(F32)).astype(BF16)
        pltpu.make_async_copy(dkvo.at[p, 0], dk_ref.at[0, :, cols(p)], out_sem).start()
        pltpu.make_async_copy(dkvo.at[p, 1], dv_ref.at[0, :, cols(p)], out_sem).start()

    y_sum(groups - 1)

    mine = pl.ds(2 * x, 2)
    wait_bytes(xr, bx_r)
    total = xsum[mine]
    for d in range(NX - 1):
        total = total + xr[d].astype(F32)
    zsend[...] = total.astype(BF16)
    xsum[mine] = total
    for d, peer in enumerate(z_peers):
        half = (z + d + 1) % NZ // ZL
        remote(zsend.at[:, 1 - half], zr.at[d], bz_s, bz_r, peer).start()
    for p in range(pairs):
        finish_keys(p)
    wait_bytes(zr, bz_r)
    total = xsum[mine, sz]
    for d in range(NZ - 1):
        total = total + zr[d].astype(F32)
    xg[x] = total
    for peer in x_peers:
        remote(xg.at[x], xg.at[x], xg_s, xg_r, peer).start()
    wait_bytes(xg.at[pl.ds(0, NX - 1)], xg_r)
    for p in range(pairs):
        rows = xg[p // 2, p % 2]
        for r in range(16):
            dp_ref[15 - r : 16 - r, p * LANES : (p + 1) * LANES] = rows[r : r + 1]

    wait_bytes(kvp, kv_s)
    wait_bytes(tab.at[:, 0, 0, 0], z_s)
    wait_bytes(tab.at[:, pl.ds(0, NY - 1), :, 0], y_s)
    wait_bytes(tab.at[:, :, :, 0], c_s)
    wait_bytes(dkv1, b_s)
    wait_bytes(corer, bc_s)
    wait_bytes(yr, by_s)
    for g in range(groups):

        @pl.when(x != g)
        def _():
            wait_bytes(xr.at[0], bx_s.at[g])

    wait_bytes(zr, bz_s)
    wait_bytes(xg.at[pl.ds(0, NX - 1)], xg_s)
    wait_bytes(inp.at[:, pl.ds(0, 3)], out_sem)


def local(query_rows, key_rows, value_rows, grad_out, pos_keys, bias_content, bias_position):
    width = query_rows.shape[2]
    pairs = width // LANES
    groups = pairs // 2
    rows = query_rows.shape
    sem = pltpu.SemaphoreType.DMA
    hbm = pl.BlockSpec(memory_space=pl.ANY)
    vmem = pl.BlockSpec(memory_space=pltpu.VMEM)
    tile = (FRAMES, LANES)
    small = (16, LANES)
    scratch = [
        pltpu.VMEM((pairs, 4, *tile), BF16),
        pltpu.VMEM((pairs, 2, *tile), BF16),
        pltpu.VMEM((pairs, NY, 2, 2, *small), BF16),
        pltpu.VMEM((pairs, *tile), BF16),
        pltpu.VMEM((pairs, 2, *tile), F32),
        pltpu.VMEM((pairs, 2, *tile), BF16),
        pltpu.VMEM((pairs, 2, *tile), BF16),
        pltpu.VMEM((pairs, 2, *tile), BF16),
        pltpu.VMEM((pairs, NY, 2, 2, *small), F32),
        pltpu.VMEM((pairs, NY, 2, 2, *small), BF16),
        pltpu.VMEM((pairs, NY, 2, *small), BF16),
        pltpu.VMEM((pairs, NY, 2, *small), BF16),
        pltpu.VMEM((NY - 1, pairs, 2, *small), BF16),
        pltpu.VMEM((pairs, 2, *small), F32),
        pltpu.VMEM((pairs, 2, *small), BF16),
        pltpu.VMEM((NX - 1, 2, 2, *small), BF16),
        pltpu.VMEM((2, 2, *small), BF16),
        pltpu.VMEM((NZ - 1, 2, *small), BF16),
        pltpu.VMEM((NX, 2, *small), F32),
        sem((pairs,)),
        sem, sem((pairs,)),
        sem, sem((groups,)),
        sem, sem((groups,)),
        sem, sem((groups,)),
        sem, sem((pairs,)),
        sem, sem((groups,)),
        sem, sem((groups,)),
        sem((groups,)), sem,
        sem, sem,
        sem, sem,
        sem,
    ]
    return pl.pallas_call(
        functools.partial(kernel, pairs),
        out_shape=(
            jax.ShapeDtypeStruct(rows, BF16),
            jax.ShapeDtypeStruct(rows, BF16),
            jax.ShapeDtypeStruct(rows, BF16),
            jax.ShapeDtypeStruct((16, width), F32),
        ),
        in_specs=[hbm, hbm, hbm, hbm, vmem, vmem, vmem],
        out_specs=(hbm, hbm, hbm, vmem),
        scratch_shapes=scratch,
        compiler_params=pltpu.CompilerParams(collective_id=0, has_side_effects=True, vmem_limit_bytes=48 << 20),
    )(
        query_rows, key_rows, value_rows, grad_out, pos_keys,
        bias_content.reshape(1, width), bias_position.reshape(1, width),
    )


def solution(mesh):
    wide = P("dp", "blk", None)
    return jax.shard_map(
        local,
        mesh=mesh,
        in_specs=(wide, wide, wide, wide, P("blk", None), P(), P()),
        out_specs=(wide, wide, wide, P("blk", None)),
        check_vma=False,
    )
```

time: 491 us -> 79.6 us (0.16)
  the two profiles are of different devices: /device:TPU:1 before, /device:TPU:2 now
where the time goes in v1:
time: 79.6 us; the launch traced here: 79.3 us
  Pallas kernels  70 us (88%)
  local copies, waits for them, and re-layouts  8.66 us (11%)
    pallas_call x1, Pallas kernels, local(): pl.pallas_call(functools.partial(kernel, pairs), out_shape=(jax.ShapeDtyp...  70 us
    unnamed x18, local copies, waits for them, and re-layouts  8.66 us

profile of v1, /device:TPU:2, one launch (start us, length us, event | category | flops | bytes accessed | tf_op | source)
XLA Modules:
  0.0 79.3 jit_solution(6332364332023950467)
XLA Ops:
  0.6 0.0 copy-start
  0.6 0.9 %copy-done = bf16[1,128,1024]{2,1,0:T(8,128)(2,1)S(1)} copy-done((bf16[1,128,1024]{2,1,0:T(8,128)(2,1)S(1)}, bf16[1,128,1024]{2,1,0:T(8,128)(2,1)}, u32[]{:S(2)}) %copy-start) | copy-done | bytes 262168
  1.6 0.0 copy-start.1
  1.6 0.9 %copy-done.1 = bf16[1,128,1024]{2,1,0:T(8,128)(2,1)S(1)} copy-done((bf16[1,128,1024]{2,1,0:T(8,128)(2,1)S(1)}, bf16[1,128,1024]{2,1,0:T(8,128)(2,1)}, u32[]{:S(2)}) %copy-start.1) | copy-done | bytes 262168
  2.5 0.0 copy-start.2
  2.5 0.9 %copy-done.2 = bf16[1,128,1024]{2,1,0:T(8,128)(2,1)S(1)} copy-done((bf16[1,128,1024]{2,1,0:T(8,128)(2,1)S(1)}, bf16[1,128,1024]{2,1,0:T(8,128)(2,1)}, u32[]{:S(2)}) %copy-start.2) | copy-done | bytes 262168
  3.5 0.0 copy-start.3
  3.5 0.9 %copy-done.3 = bf16[1,128,1024]{2,1,0:T(8,128)(2,1)S(1)} copy-done((bf16[1,128,1024]{2,1,0:T(8,128)(2,1)S(1)}, bf16[1,128,1024]{2,1,0:T(8,128)(2,1)}, u32[]{:S(2)}) %copy-start.3) | copy-done | bytes 262168
  4.4 0.0 copy-start.4
  4.4 0.8 copy-done.4
  5.2 0.0 copy-start.5
  5.2 0.7 copy-done.5
  5.9 0.0 copy-start.6
  5.9 0.7 copy-done.6
  6.6 70.0 %shard_map.102 = (bf16[1,128,1024]{2,1,0:T(8,128)(2,1)S(1)}, bf16[1,128,1024]{2,1,0:T(8,128)(2,1)S(1)}, bf16[1,128,1024]{2,1,0:T(8,128)(2,1)S(1)}, f32[16,1024]{1,0:T(8,128)S(1)}) custom-call(bf16[1,128,1024]{2,1,0:T(8,128)(2,1)S(1)} %copy-done, bf16[1,128,1024]{2,1,0:T(8,128)(2,1)S(1)} %copy-done.1, bf16[1,128,1024]{2,1,0:T(8,128)(2,1)S(1)} %copy-done.2, ...), custom_call_target="tpu_custom_call" | custom-call | tf_op jit(solution)/shard_map/pallas_call | solution.py:334
  76.5 0.7 copy.15
  77.2 0.7 copy.16
  77.9 0.7 copy.17
  78.6 0.6 copy.18
Async XLA Ops:
  0.6 1.0 %copy-start = (bf16[1,128,1024]{2,1,0:T(8,128)(2,1)S(1)}, bf16[1,128,1024]{2,1,0:T(8,128)(2,1)}, u32[]{:S(2)}) copy-start(bf16[1,128,1024]{2,1,0:T(8,128)(2,1)} %q_ref.1) | copy-start | bytes 786436
  1.6 0.9 %copy-start.1 = (bf16[1,128,1024]{2,1,0:T(8,128)(2,1)S(1)}, bf16[1,128,1024]{2,1,0:T(8,128)(2,1)}, u32[]{:S(2)}) copy-start(bf16[1,128,1024]{2,1,0:T(8,128)(2,1)} %k_ref.1) | copy-start | bytes 786436
  2.5 0.9 %copy-start.2 = (bf16[1,128,1024]{2,1,0:T(8,128)(2,1)S(1)}, bf16[1,128,1024]{2,1,0:T(8,128)(2,1)}, u32[]{:S(2)}) copy-start(bf16[1,128,1024]{2,1,0:T(8,128)(2,1)} %v_ref.1) | copy-start | bytes 786436
  3.5 0.9 %copy-start.3 = (bf16[1,128,1024]{2,1,0:T(8,128)(2,1)S(1)}, bf16[1,128,1024]{2,1,0:T(8,128)(2,1)}, u32[]{:S(2)}) copy-start(bf16[1,128,1024]{2,1,0:T(8,128)(2,1)} %g_ref.1) | copy-start | bytes 786436
  4.4 0.8 copy-start.4
  5.2 0.7 copy-start.5
  5.9 0.7 copy-start.6

commit v2 on v1

v2 whole, which is shorter than its diff:
```python
import functools

import jax
import jax.numpy as jnp
from jax import lax
from jax.experimental import pallas as pl
from jax.experimental.pallas import tpu as pltpu
from jax.sharding import PartitionSpec as P

MESH = pl.DeviceIdType.MESH
DH = 64
LANES = 2 * DH
FRAMES = 128
F32, BF16 = jnp.float32, jnp.bfloat16
NX, NY, NZ, ZL = 4, 8, 8, 4
QUERY, GRAD, KEY, VALUE = range(4)
GATHER = ((0, 1), (1, 1), (2, 2), (4, 2), (6, 2))
REDUCE = ((0, 2), (2, 2), (4, 2), (6, 1), (7, 1))


def contract_lanes(a, b):
    return lax.dot_general(a, b, (((1,), (1,)), ((), ())), preferred_element_type=F32)


def contract_rows(a, b):
    return lax.dot_general(a, b, (((0,), (0,)), ((), ())), preferred_element_type=F32)


def place_roll(x):
    rows = x.shape[0]
    blocks = [
        pltpu.roll(x[8 * a : 8 * a + 8], (127 - 8 * a) % 128, 1) for a in range(rows // 8)
    ]
    x = jnp.concatenate(blocks, axis=0)
    row = lax.broadcasted_iota(jnp.int32, x.shape, 0)
    for bit in range(3):
        moved = pltpu.roll(x, 128 - 2**bit, 1)
        x = jnp.where(((row >> bit) & 1) == 1, moved, x)
    return x


def pair_grads(q, grad, keys, values, table, bias_c, bias_p):
    first = lax.broadcasted_iota(jnp.int32, (FRAMES, LANES), 1) < DH

    def stacked(x):
        zero = jnp.zeros_like(x)
        both = jnp.concatenate([jnp.where(first, x, zero), jnp.where(first, zero, x)], axis=0)
        return both.astype(BF16)

    q32 = q.astype(F32)
    content_in = stacked(q32 + bias_c)
    position_in = stacked(q32 + bias_p)
    grad_in = stacked(grad.astype(F32))
    content = contract_lanes(content_in, keys)
    spread = contract_lanes(position_in, table)
    weights = contract_lanes(grad_in, values)
    shape = (2 * FRAMES, FRAMES)
    frame = lax.broadcasted_iota(jnp.int32, shape, 0) & (FRAMES - 1)
    upper = lax.broadcasted_iota(jnp.int32, shape, 1) + frame >= FRAMES - 1

    def select(at):
        picked = jnp.where(upper, spread[:, at : at + 128], spread[:, at + 128 : at + 256])
        return pltpu.roll(picked, 1, 1, stride=1, stride_axis=0)

    factor = DH**-0.5
    s0 = (content[:, :128] + select(256)) * factor
    s1 = (content[:, 128:] + select(0)) * factor
    top = jnp.max(jnp.maximum(s0, s1), axis=1, keepdims=True)
    e0, e1 = jnp.exp(s0 - top), jnp.exp(s1 - top)
    inverse = 1.0 / jnp.sum(e0 + e1, axis=1, keepdims=True)
    a0, a1 = e0 * inverse, e1 * inverse
    w0, w1 = weights[:, :128], weights[:, 128:]
    delta = jnp.sum(a0 * w0 + a1 * w1, axis=1, keepdims=True)
    d0 = a0 * (w0 - delta) * factor
    d1 = a1 * (w1 - delta) * factor
    dscore = jnp.concatenate([d0, d1], axis=1).astype(BF16)
    attention = jnp.concatenate([a0, a1], axis=1).astype(BF16)
    p0, p1 = place_roll(d0), place_roll(d1)
    zero = jnp.zeros_like(p0)
    location = jnp.concatenate(
        [
            jnp.where(upper, p1, zero),
            jnp.where(upper, zero, p1),
            jnp.where(upper, p0, zero),
            jnp.where(upper, zero, p0),
        ],
        axis=1,
    ).astype(BF16)
    both = jnp.dot(
        jnp.concatenate([dscore, location], axis=1),
        jnp.concatenate([keys, table], axis=0),
        preferred_element_type=F32,
    )
    query_gradient = jnp.where(first, both[:FRAMES], both[FRAMES:])
    key_term = contract_rows(dscore, content_in)
    value_term = contract_rows(attention, grad_in)
    band_term = contract_rows(location, position_in)
    return query_gradient, key_term, value_term, band_term


def kernel(
    pairs,
    q_ref, k_ref, v_ref, g_ref, pos_ref, bc_ref, bp_ref,
    dq_ref, dk_ref, dv_ref, dp_ref,
    dqv, dkvo, inp, posv, biases, kvp, tab, dkv0, dkv1, dkv1r, band, band16, corer, ysend, yr, xr, zown, zr,
    in_sem, first_sem, kv_s, kv_r, z_s, z_r, y_s, y_r, c_s, c_r, b_s, b_r, bc_s, bc_r, by_s, by_r, bx_s, bx_r, bz_s, bz_r, out_sem,
):
    dp, blk = lax.axis_index("dp"), lax.axis_index("blk")
    x, zl = dp // ZL, dp % ZL
    y, zh, c = blk // 4, (blk // 2) % 2, blk % 2
    z = zh * ZL + zl
    count = 4 * NY

    def at(x_, y_, z_, c_):
        return (x_ * ZL + z_ % ZL, (y_ * 2 + z_ // ZL) * 2 + c_)

    following, before = (dp, (blk + 1) % count), (dp, (blk + count - 1) % count)
    partner = at(x, y, z, 1 - c)
    opposite = (dp, (y * 2 + 1 - zh) * 2 + c)
    y_peers = [at(x, (y + d) % NY, z, c) for d in range(1, NY)]
    x_peers = [at((x + d) % NX, y, z, c) for d in range(1, NX)]
    z_peers = [at(x, y, (z + d) % NZ, c) for d in range(1, NZ)]
    y_order = (3, 2, 4, 1, 5, 0, 6)

    def remote(src, dst, send, recv, device):
        return pltpu.make_async_remote_copy(
            src_ref=src, dst_ref=dst, send_sem=send, recv_sem=recv, device_id=device, device_id_type=MESH
        )

    def wait_bytes(ref, sem):
        pltpu.make_async_copy(ref, ref, sem).wait()

    def cols(p):
        return pl.ds(p * LANES, LANES)

    def chunk(k, chunks):
        return pl.ds(*chunks[k])

    barrier = pltpu.get_barrier_semaphore()
    peers = [following, before] + y_peers + x_peers + z_peers
    for peer in peers:
        pl.semaphore_signal(barrier, inc=1, device_id=peer, device_id_type=MESH)
    pos_copy = pltpu.make_async_copy(pos_ref, posv, first_sem.at[0])
    pos_copy.start()
    bias_copies = [
        pltpu.make_async_copy(ref, biases.at[n], first_sem.at[1 + n]) for n, ref in enumerate((bc_ref, bp_ref))
    ]
    for copy in bias_copies:
        copy.start()
    for p in range(pairs):
        for n, ref in ((QUERY, q_ref), (GRAD, g_ref), (KEY, k_ref), (VALUE, v_ref)):
            pltpu.make_async_copy(ref.at[0, :, cols(p)], inp.at[p, n], in_sem.at[p]).start()

    flip = (
        lax.broadcasted_iota(jnp.int32, (16, 16), 0) + lax.broadcasted_iota(jnp.int32, (16, 16), 1) == 15
    )
    pos_copy.wait()
    turned = jnp.dot(
        jnp.where(flip, 1.0, 0.0).astype(BF16), posv[...], preferred_element_type=F32
    ).astype(BF16)
    sy, sz, sc = NY - 1 - y, 1 - zh, 1 - c
    for p in range(pairs):
        tab[p, sy, sz, sc] = turned[:, p * LANES : (p + 1) * LANES]
    for copy in bias_copies:
        copy.wait()
    pl.semaphore_wait(barrier, len(peers))

    def shard(k, z_):
        return tab.at[chunk(k, GATHER), sy, z_, sc]

    def along_y(k, z_):
        for d in y_order:
            remote(shard(k, z_), shard(k, z_), y_s, y_r.at[k], y_peers[d]).start()

    def shift(k):
        for p in range(GATHER[k][0], sum(GATHER[k])):
            for n, ref in ((0, k_ref), (1, v_ref)):
                remote(ref.at[0, :, cols(p)], kvp.at[p, n], kv_s, kv_r.at[p], following).start()

    chunks = len(GATHER)
    for k in range(chunks):
        remote(shard(k, sz), shard(k, sz), z_s, z_r.at[k], opposite).start()
    for k in range(chunks):
        shift(k)
        if k < chunks - 1:
            along_y(k, sz)
    for k in range(chunks):
        wait_bytes(shard(k, 1 - sz), z_r.at[k])
        along_y(k, 1 - sz)
        if k == 1:
            along_y(chunks - 1, sz)

    def share_table(k):
        wait_bytes(tab.at[chunk(k, GATHER), pl.ds(0, NY - 1), :, 0], y_r.at[k])
        mine = tab.at[chunk(k, GATHER), :, :, sc]
        remote(mine, mine, c_s, c_r.at[k], partner).start()

    def pair_step(p):
        wait_bytes(inp.at[p], in_sem.at[p])
        wait_bytes(kvp.at[p], kv_r.at[p])
        keys = jnp.concatenate([inp[p, KEY], kvp[p, 0]], axis=0)
        values = jnp.concatenate([inp[p, VALUE], kvp[p, 1]], axis=0)
        table = tab[p].reshape(32 * 16, LANES)
        lanes = slice(p * LANES, (p + 1) * LANES)
        dq, dk, dv, db = pair_grads(
            inp[p, QUERY], inp[p, GRAD], keys, values, table, biases[0, :, lanes], biases[1, :, lanes]
        )
        dqv[p] = dq.astype(BF16)
        pltpu.make_async_copy(dqv.at[p], dq_ref.at[0, :, cols(p)], out_sem.at[0]).start()
        dkv0[p, 0] = dk[:FRAMES]
        dkv0[p, 1] = dv[:FRAMES]
        dkv1[p, 0] = dk[FRAMES:].astype(BF16)
        dkv1[p, 1] = dv[FRAMES:].astype(BF16)
        db = db.reshape(NY, 2, 2, 16, LANES)
        band[p] = db
        band16[p] = db.astype(BF16)

    def send_back(k):
        part = chunk(k, REDUCE)
        remote(band16.at[part, :, :, c], corer.at[part], bc_s, bc_r.at[k], partner).start()
        for p in range(REDUCE[k][0], sum(REDUCE[k])):
            remote(dkv1.at[p], dkv1r.at[p], b_s, b_r.at[p], before).start()

    def chip_sum(k):
        part = chunk(k, REDUCE)
        wait_bytes(corer.at[part], bc_r.at[k])
        for p in range(REDUCE[k][0], sum(REDUCE[k])):
            total = band[p, :, :, sc] + corer[p].astype(F32)
            ysend[p] = total.astype(BF16)
        for d in y_order:
            sink = NY - 1 - (y + d + 1) % NY
            remote(ysend.at[part, sink], yr.at[d, part], by_s, by_r.at[k], y_peers[d]).start()

    def y_sum(k):
        part = chunk(k, REDUCE)
        wait_bytes(yr.at[:, part], by_r.at[k])
        for p in range(REDUCE[k][0], sum(REDUCE[k])):
            total = band[p, sy, :, sc] + corer[p, sy].astype(F32)
            for d in range(NY - 1):
                total = total + yr[d, p].astype(F32)
            xr[x, p] = total.astype(BF16)
        for peer in x_peers:
            remote(xr.at[x, part], xr.at[x, part], bx_s, bx_r.at[k], peer).start()

    def x_sum(k):
        part = chunk(k, REDUCE)
        wait_bytes(xr.at[pl.ds(0, NX - 1), part], bx_r.at[k])
        for p in range(REDUCE[k][0], sum(REDUCE[k])):
            total = xr[0, p].astype(F32)
            for d in range(1, NX):
                total = total + xr[d, p].astype(F32)
            zown[p] = total.astype(BF16)
            zr[z, p] = zown[p, sz]
        for d, peer in enumerate(z_peers):
            half = (z + d + 1) % NZ // ZL
            remote(zown.at[part, 1 - half], zr.at[z, part], bz_s, bz_r, peer).start()

    def finish_keys(p):
        wait_bytes(dkv1r.at[p], b_r.at[p])
        dkvo[p] = (dkv0[p] + dkv1r[p].astype(F32)).astype(BF16)
        for n, ref in ((0, dk_ref), (1, dv_ref)):
            pltpu.make_async_copy(dkvo.at[p, n], ref.at[0, :, cols(p)], out_sem.at[1]).start()

    done = 0
    share_table(0)
    for k, (start, number) in enumerate(GATHER):
        wait_bytes(tab.at[chunk(k, GATHER), :, :, 0], c_r.at[k])
        for p in range(start, start + number):
            pair_step(p)
            if p == start and k + 1 < chunks:
                share_table(k + 1)
            if p + 1 == sum(REDUCE[done]):
                send_back(done)
                if done >= 1:
                    chip_sum(done - 1)
                done += 1
    last = len(REDUCE) - 1
    y_sum(0)
    chip_sum(last)
    for k in range(1, last):
        y_sum(k)
        x_sum(k - 1)
    for p in range(pairs - 2):
        finish_keys(p)
    y_sum(last)
    x_sum(last - 1)
    x_sum(last)
    for p in range(pairs - 2, pairs):
        finish_keys(p)
    wait_bytes(zr.at[pl.ds(0, NZ - 1)], bz_r)
    for p in range(pairs):
        total = zr[0, p].astype(F32)
        for d in range(1, NZ):
            total = total + zr[d, p].astype(F32)
        for r in range(16):
            dp_ref[15 - r : 16 - r, p * LANES : (p + 1) * LANES] = total[r : r + 1]

    wait_bytes(kvp, kv_s)
    wait_bytes(tab.at[:, 0, 0, 0], z_s)
    wait_bytes(tab.at[:, pl.ds(0, NY - 1), :, 0], y_s)
    wait_bytes(tab.at[:, :, :, 0], c_s)
    wait_bytes(dkv1, b_s)
    wait_bytes(corer, bc_s)
    wait_bytes(yr, by_s)
    wait_bytes(xr.at[pl.ds(0, NX - 1)], bx_s)
    wait_bytes(zr.at[pl.ds(0, NZ - 1)], bz_s)
    wait_bytes(dqv, out_sem.at[0])
    wait_bytes(dkvo, out_sem.at[1])


def write_out(*refs):
    sources, results, held, sems = refs[:4], refs[4:8], refs[8:12], refs[12]
    loads = [pltpu.make_async_copy(a, b, sems.at[0, n]) for n, (a, b) in enumerate(zip(sources, held))]
    stores = [pltpu.make_async_copy(a, b, sems.at[1, n]) for n, (a, b) in enumerate(zip(held, results))]
    for copy in loads:
        copy.start()
    for load, store in zip(loads, stores):
        load.wait()
        store.start()
    for copy in stores:
        copy.wait()


def local(query_rows, key_rows, value_rows, grad_out, pos_keys, bias_content, bias_position):
    width = query_rows.shape[2]
    pairs = width // LANES
    rows = query_rows.shape
    sem = pltpu.SemaphoreType.DMA
    hbm = pl.BlockSpec(memory_space=pltpu.HBM)
    vmem = pl.BlockSpec(memory_space=pltpu.VMEM)
    tile = (FRAMES, LANES)
    small = (16, LANES)
    gather, reduce = sem((len(GATHER),)), sem((len(REDUCE),))
    scratch = [
        pltpu.VMEM((pairs, *tile), BF16),
        pltpu.VMEM((pairs, 2, *tile), BF16),
        pltpu.VMEM((pairs, 4, *tile), BF16),
        pltpu.VMEM((16, width), BF16),
        pltpu.VMEM((2, 1, width), F32),
        pltpu.VMEM((pairs, 2, *tile), BF16),
        pltpu.VMEM((pairs, NY, 2, 2, *small), BF16),
        pltpu.VMEM((pairs, 2, *tile), F32),
        pltpu.VMEM((pairs, 2, *tile), BF16),
        pltpu.VMEM((pairs, 2, *tile), BF16),
        pltpu.VMEM((pairs, NY, 2, 2, *small), F32),
        pltpu.VMEM((pairs, NY, 2, 2, *small), BF16),
        pltpu.VMEM((pairs, NY, 2, *small), BF16),
        pltpu.VMEM((pairs, NY, 2, *small), BF16),
        pltpu.VMEM((NY - 1, pairs, 2, *small), BF16),
        pltpu.VMEM((NX, pairs, 2, *small), BF16),
        pltpu.VMEM((pairs, 2, *small), BF16),
        pltpu.VMEM((NZ, pairs, *small), BF16),
        sem((pairs,)),
        sem((3,)),
        sem, sem((pairs,)),
        sem, gather,
        sem, gather,
        sem, gather,
        sem, sem((pairs,)),
        sem, reduce,
        sem, reduce,
        sem, reduce,
        sem, sem,
        sem((2,)),
    ]
    wide = jax.ShapeDtypeStruct(rows, BF16)
    results = (wide, wide, wide, jax.ShapeDtypeStruct((16, width), F32))
    raw = pl.pallas_call(
        functools.partial(kernel, pairs),
        out_shape=results,
        in_specs=[hbm] * 7,
        out_specs=(hbm, hbm, hbm, vmem),
        scratch_shapes=scratch,
        compiler_params=pltpu.CompilerParams(
            collective_id=0, has_side_effects=True, vmem_limit_bytes=67_043_328
        ),
    )(
        query_rows, key_rows, value_rows, grad_out, pos_keys,
        bias_content.reshape(1, width), bias_position.reshape(1, width),
    )
    return pl.pallas_call(
        write_out,
        out_shape=results,
        in_specs=[hbm] * 4,
        out_specs=(hbm,) * 4,
        scratch_shapes=[pltpu.VMEM(a.shape, a.dtype) for a in results] + [sem((2, 4))],
        compiler_params=pltpu.CompilerParams(vmem_limit_bytes=67_043_328),
    )(*raw)


def solution(mesh):
    wide = P("dp", "blk", None)
    return jax.shard_map(
        local,
        mesh=mesh,
        in_specs=(wide, wide, wide, wide, P("blk", None), P(), P()),
        out_specs=(wide, wide, wide, P("blk", None)),
        check_vma=False,
    )
```

time: 79.6 us -> 70.4 us (0.88)
  local copies, waits for them, and re-layouts: 8.66 us -> 0 us
    unnamed x18 -> x0, local copies, waits for them, and re-layouts: 8.66 us -> none
    pallas_call x1 -> x2, Pallas kernels: 70 us -> 69.5 us  [the longest x1 67.6 us: local(): pl.pallas_call(functools.partial(kernel, pairs), out_shape=results, in_sp...]
where the time goes in v2:
time: 70.4 us; the launch traced here: 70.2 us
  Pallas kernels  69.5 us (99%)
    pallas_call x1, Pallas kernels, local(): pl.pallas_call(functools.partial(kernel, pairs), out_shape=results, in_sp...  67.6 us
    pallas_call x1, Pallas kernels, local(): pl.pallas_call(write_out, out_shape=results, in_specs=[hbm] * 4, out_spec...  1.91 us

profile of v2, /device:TPU:2, one launch (start us, length us, event | category | flops | bytes accessed | tf_op | source)
XLA Modules:
  0.0 70.2 jit_solution(3920420065330324731)
XLA Ops:
  0.6 67.6 %shard_map.102 = (bf16[1,128,1024]{2,1,0:T(8,128)(2,1)}, bf16[1,128,1024]{2,1,0:T(8,128)(2,1)}, bf16[1,128,1024]{2,1,0:T(8,128)(2,1)}, f32[16,1024]{1,0:T(8,128)}) custom-call(bf16[1,128,1024]{2,1,0:T(8,128)(2,1)} %q_ref.1, bf16[1,128,1024]{2,1,0:T(8,128)(2,1)} %k_ref.1, bf16[1,128,1024]{2,1,0:T(8,128)(2,1)} %v_ref.1, bf16[1,128,1024]{2,1,0:T(8,128)(2,1)} %g_ref.1, ...), custom_call_target="tpu_custom_call" | custom-call | tf_op jit(solution)/shard_map/pallas_call | solution.py:368
  68.3 1.9 %shard_map.103 = (bf16[1,128,1024]{2,1,0:T(8,128)(2,1)}, bf16[1,128,1024]{2,1,0:T(8,128)(2,1)}, bf16[1,128,1024]{2,1,0:T(8,128)(2,1)}, f32[16,1024]{1,0:T(8,128)}) custom-call(bf16[1,128,1024]{2,1,0:T(8,128)(2,1)} %get-tuple-element.8.refs_0_, bf16[1,128,1024]{2,1,0:T(8,128)(2,1)} %get-tuple-element.9.refs_1_, ...), custom_call_target="tpu_custom_call" | custom-call | tf_op jit(solution)/shard_map/pallas_call | solution.py:381

commit v3 on v2

--- a/solution.py
+++ b/solution.py
@@ -26,17 +26,21 @@
     return lax.dot_general(a, b, (((0,), (0,)), ((), ())), preferred_element_type=F32)
 
 
-def place_roll(x):
-    rows = x.shape[0]
-    blocks = [
-        pltpu.roll(x[8 * a : 8 * a + 8], (127 - 8 * a) % 128, 1) for a in range(rows // 8)
-    ]
-    x = jnp.concatenate(blocks, axis=0)
-    row = lax.broadcasted_iota(jnp.int32, x.shape, 0)
-    for bit in range(3):
-        moved = pltpu.roll(x, 128 - 2**bit, 1)
-        x = jnp.where(((row >> bit) & 1) == 1, moved, x)
-    return x
+def place_roll(d):
+    rows = d.shape[0]
+    shape = (FRAMES, FRAMES)
+    flip = lax.broadcasted_iota(jnp.int32, shape, 0) + lax.broadcasted_iota(jnp.int32, shape, 1) == FRAMES - 1
+    flip = jnp.where(flip, 1.0, 0.0).astype(BF16)
+
+    def turned(m):
+        return jnp.concatenate(
+            [jnp.dot(flip, m[at : at + FRAMES], preferred_element_type=F32) for at in range(0, rows, FRAMES)], axis=0
+        )
+
+    upside = turned(d)
+    rolled = [pltpu.roll(upside[:, at : at + FRAMES], 0, 1, stride=1, stride_axis=0) for at in (0, FRAMES)]
+    placed = turned(jnp.concatenate(rolled, axis=1).astype(BF16)).astype(BF16)
+    return placed[:, :FRAMES], placed[:, FRAMES:]
 
 
 def pair_grads(q, grad, keys, values, table, bias_c, bias_p):
@@ -75,7 +79,7 @@
     d1 = a1 * (w1 - delta) * factor
     dscore = jnp.concatenate([d0, d1], axis=1).astype(BF16)
     attention = jnp.concatenate([a0, a1], axis=1).astype(BF16)
-    p0, p1 = place_roll(d0), place_roll(d1)
+    p0, p1 = place_roll(dscore)
     zero = jnp.zeros_like(p0)
     location = jnp.concatenate(
         [
@@ -85,7 +89,7 @@
             jnp.where(upper, zero, p0),
         ],
         axis=1,
-    ).astype(BF16)
+    )
     both = jnp.dot(
         jnp.concatenate([dscore, location], axis=1),
         jnp.concatenate([keys, table], axis=0),
@@ -147,9 +151,6 @@
     ]
     for copy in bias_copies:
         copy.start()
-    for p in range(pairs):
-        for n, ref in ((QUERY, q_ref), (GRAD, g_ref), (KEY, k_ref), (VALUE, v_ref)):
-            pltpu.make_async_copy(ref.at[0, :, cols(p)], inp.at[p, n], in_sem.at[p]).start()
 
     flip = (
         lax.broadcasted_iota(jnp.int32, (16, 16), 0) + lax.broadcasted_iota(jnp.int32, (16, 16), 1) == 15
@@ -178,17 +179,26 @@
                 remote(ref.at[0, :, cols(p)], kvp.at[p, n], kv_s, kv_r.at[p], following).start()
 
     chunks = len(GATHER)
+
+    def pass_on(k):
+        wait_bytes(shard(k, 1 - sz), z_r.at[k])
+        along_y(k, 1 - sz)
+
     for k in range(chunks):
         remote(shard(k, sz), shard(k, sz), z_s, z_r.at[k], opposite).start()
-    for k in range(chunks):
+    for k in (0, 1):
+        along_y(k, sz)
         shift(k)
-        if k < chunks - 1:
-            along_y(k, sz)
-    for k in range(chunks):
-        wait_bytes(shard(k, 1 - sz), z_r.at[k])
-        along_y(k, 1 - sz)
-        if k == 1:
-            along_y(chunks - 1, sz)
+    along_y(2, sz)
+    for p in range(pairs):
+        for n, ref in ((QUERY, q_ref), (GRAD, g_ref), (KEY, k_ref), (VALUE, v_ref)):
+            pltpu.make_async_copy(ref.at[0, :, cols(p)], inp.at[p, n], in_sem.at[p]).start()
+    pass_on(0)
+    pass_on(1)
+    shift(2)
+    pass_on(2)
+    along_y(3, sz)
+    shift(3)
 
     def share_table(k):
         wait_bytes(tab.at[chunk(k, GATHER), pl.ds(0, NY - 1), :, 0], y_r.at[k])
@@ -263,12 +273,17 @@
 
     done = 0
     share_table(0)
+    pass_on(3)
+    share_table(1)
+    along_y(4, sz)
+    pass_on(4)
+    shift(4)
     for k, (start, number) in enumerate(GATHER):
         wait_bytes(tab.at[chunk(k, GATHER), :, :, 0], c_r.at[k])
         for p in range(start, start + number):
             pair_step(p)
-            if p == start and k + 1 < chunks:
-                share_table(k + 1)
+            if p == start and k + 2 < chunks:
+                share_table(k + 2)
             if p + 1 == sum(REDUCE[done]):
                 send_back(done)
                 if done >= 1:
@@ -277,13 +292,16 @@
     last = len(REDUCE) - 1
     y_sum(0)
     chip_sum(last)
-    for k in range(1, last):
-        y_sum(k)
-        x_sum(k - 1)
+    y_sum(1)
+    x_sum(0)
+    y_sum(2)
+    y_sum(3)
+    x_sum(1)
+    y_sum(last)
+    x_sum(2)
+    x_sum(3)
     for p in range(pairs - 2):
         finish_keys(p)
-    y_sum(last)
-    x_sum(last - 1)
     x_sum(last)
     for p in range(pairs - 2, pairs):
         finish_keys(p)

time: 70.4 us -> 62 us (0.88)
  the two profiles are of different devices: /device:TPU:2 before, /device:TPU:8 now
where the time goes in v3:
time: 62 us; the launch traced here: 61.8 us
  Pallas kernels  61.2 us (99%)
  between operations  0.64 us (1%)
    pallas_call x1, Pallas kernels, local(): pl.pallas_call(functools.partial(kernel, pairs), out_shape=results, in_sp...  59.3 us
    pallas_call x1, Pallas kernels, local(): pl.pallas_call(write_out, out_shape=results, in_specs=[hbm] * 4, out_spec...  1.91 us

profile of v3, /device:TPU:8, one launch (start us, length us, event | category | flops | bytes accessed | tf_op | source)
XLA Modules:
  0.0 61.8 jit_solution(12912453403738044450)
XLA Ops:
  0.6 59.3 %shard_map.102 = (bf16[1,128,1024]{2,1,0:T(8,128)(2,1)}, bf16[1,128,1024]{2,1,0:T(8,128)(2,1)}, bf16[1,128,1024]{2,1,0:T(8,128)(2,1)}, f32[16,1024]{1,0:T(8,128)}) custom-call(bf16[1,128,1024]{2,1,0:T(8,128)(2,1)} %q_ref.1, bf16[1,128,1024]{2,1,0:T(8,128)(2,1)} %k_ref.1, bf16[1,128,1024]{2,1,0:T(8,128)(2,1)} %v_ref.1, bf16[1,128,1024]{2,1,0:T(8,128)(2,1)} %g_ref.1, ...), custom_call_target="tpu_custom_call" | custom-call | tf_op jit(solution)/shard_map/pallas_call | solution.py:386
  59.9 1.9 %shard_map.103 = (bf16[1,128,1024]{2,1,0:T(8,128)(2,1)}, bf16[1,128,1024]{2,1,0:T(8,128)(2,1)}, bf16[1,128,1024]{2,1,0:T(8,128)(2,1)}, f32[16,1024]{1,0:T(8,128)}) custom-call(bf16[1,128,1024]{2,1,0:T(8,128)(2,1)} %get-tuple-element.8.refs_0_, bf16[1,128,1024]{2,1,0:T(8,128)(2,1)} %get-tuple-element.9.refs_1_, ...), custom_call_target="tpu_custom_call" | custom-call | tf_op jit(solution)/shard_map/pallas_call | solution.py:399

commit v4 on v3

--- a/solution.py
+++ b/solution.py
@@ -15,7 +15,10 @@
 NX, NY, NZ, ZL = 4, 8, 8, 4
 QUERY, GRAD, KEY, VALUE = range(4)
 GATHER = ((0, 1), (1, 1), (2, 2), (4, 2), (6, 2))
-REDUCE = ((0, 2), (2, 2), (4, 2), (6, 1), (7, 1))
+SPLIT = 3
+LAG = 1
+TOGETHER = ((0,), (1,), (2,), (3,), (4, 5), (6,), (7,))
+REDUCE = ((0, 2), (2, 1), (3, 1), (4, 1), (5, 1), (6, 1), (7, 1))
 
 
 def contract_lanes(a, b):
@@ -107,7 +110,7 @@
     q_ref, k_ref, v_ref, g_ref, pos_ref, bc_ref, bp_ref,
     dq_ref, dk_ref, dv_ref, dp_ref,
     dqv, dkvo, inp, posv, biases, kvp, tab, dkv0, dkv1, dkv1r, band, band16, corer, ysend, yr, xr, zown, zr,
-    in_sem, first_sem, kv_s, kv_r, z_s, z_r, y_s, y_r, c_s, c_r, b_s, b_r, bc_s, bc_r, by_s, by_r, bx_s, bx_r, bz_s, bz_r, out_sem,
+    in_sem, first_sem, kv_s, kv_r, z_s, z_r, y_s, y_r, h_s, h_r, c_s, c_r, b_s, b_r, bc_s, bc_r, by_s, by_r, bx_s, bx_r, bz_s, bz_r, out_sem,
 ):
     dp, blk = lax.axis_index("dp"), lax.axis_index("blk")
     x, zl = dp // ZL, dp % ZL
@@ -160,14 +163,27 @@
         jnp.where(flip, 1.0, 0.0).astype(BF16), posv[...], preferred_element_type=F32
     ).astype(BF16)
     sy, sz, sc = NY - 1 - y, 1 - zh, 1 - c
+    split_from = GATHER[SPLIT][0]
     for p in range(pairs):
-        tab[p, sy, sz, sc] = turned[:, p * LANES : (p + 1) * LANES]
+        rows = turned[:, p * LANES : (p + 1) * LANES]
+        if p < split_from:
+            tab[p, sy, sz, sc] = rows
+        else:
+
+            @pl.when(x == p - split_from)
+            def _(p=p, rows=rows):
+                tab[p, sy, sz, sc] = rows
     for copy in bias_copies:
         copy.wait()
     pl.semaphore_wait(barrier, len(peers))
 
+    own_pair = pl.ds(GATHER[SPLIT][0] + x, 1)
+
+    def gathered(k):
+        return own_pair if k == SPLIT else chunk(k, GATHER)
+
     def shard(k, z_):
-        return tab.at[chunk(k, GATHER), sy, z_, sc]
+        return tab.at[gathered(k), sy, z_, sc]
 
     def along_y(k, z_):
         for d in y_order:
@@ -184,46 +200,56 @@
         wait_bytes(shard(k, 1 - sz), z_r.at[k])
         along_y(k, 1 - sz)
 
-    for k in range(chunks):
+    for k in range(SPLIT + 1):
         remote(shard(k, sz), shard(k, sz), z_s, z_r.at[k], opposite).start()
     for k in (0, 1):
         along_y(k, sz)
         shift(k)
+    along_y(SPLIT, sz)
     along_y(2, sz)
     for p in range(pairs):
         for n, ref in ((QUERY, q_ref), (GRAD, g_ref), (KEY, k_ref), (VALUE, v_ref)):
             pltpu.make_async_copy(ref.at[0, :, cols(p)], inp.at[p, n], in_sem.at[p]).start()
-    pass_on(0)
-    pass_on(1)
-    shift(2)
-    pass_on(2)
-    along_y(3, sz)
-    shift(3)
+    for k in (0, 1, SPLIT, 2):
+        pass_on(k)
+    for k in range(2, chunks):
+        shift(k)
+
+    def gather_wait(k):
+        wait_bytes(tab.at[gathered(k), pl.ds(0, NY - 1), :, 0], y_r.at[k])
+
+    def hand_round():
+        gather_wait(SPLIT)
+        rows = tab.at[own_pair, :, :, sc]
+        for peer in x_peers:
+            remote(rows, rows, h_s, h_r, peer).start()
 
     def share_table(k):
-        wait_bytes(tab.at[chunk(k, GATHER), pl.ds(0, NY - 1), :, 0], y_r.at[k])
         mine = tab.at[chunk(k, GATHER), :, :, sc]
         remote(mine, mine, c_s, c_r.at[k], partner).start()
 
-    def pair_step(p):
-        wait_bytes(inp.at[p], in_sem.at[p])
-        wait_bytes(kvp.at[p], kv_r.at[p])
-        keys = jnp.concatenate([inp[p, KEY], kvp[p, 0]], axis=0)
-        values = jnp.concatenate([inp[p, VALUE], kvp[p, 1]], axis=0)
-        table = tab[p].reshape(32 * 16, LANES)
-        lanes = slice(p * LANES, (p + 1) * LANES)
-        dq, dk, dv, db = pair_grads(
-            inp[p, QUERY], inp[p, GRAD], keys, values, table, biases[0, :, lanes], biases[1, :, lanes]
-        )
-        dqv[p] = dq.astype(BF16)
-        pltpu.make_async_copy(dqv.at[p], dq_ref.at[0, :, cols(p)], out_sem.at[0]).start()
-        dkv0[p, 0] = dk[:FRAMES]
-        dkv0[p, 1] = dv[:FRAMES]
-        dkv1[p, 0] = dk[FRAMES:].astype(BF16)
-        dkv1[p, 1] = dv[FRAMES:].astype(BF16)
-        db = db.reshape(NY, 2, 2, 16, LANES)
-        band[p] = db
-        band16[p] = db.astype(BF16)
+    def pair_steps(*ps):
+        for p in ps:
+            wait_bytes(inp.at[p], in_sem.at[p])
+            wait_bytes(kvp.at[p], kv_r.at[p])
+        for p in ps:
+            keys = jnp.concatenate([inp[p, KEY], kvp[p, 0]], axis=0)
+            values = jnp.concatenate([inp[p, VALUE], kvp[p, 1]], axis=0)
+            table = tab[p].reshape(32 * 16, LANES)
+            lanes = slice(p * LANES, (p + 1) * LANES)
+            dq, dk, dv, db = pair_grads(
+                inp[p, QUERY], inp[p, GRAD], keys, values, table, biases[0, :, lanes], biases[1, :, lanes]
+            )
+            dqv[p] = dq.astype(BF16)
+            dkv0[p, 0] = dk[:FRAMES]
+            dkv0[p, 1] = dv[:FRAMES]
+            dkv1[p, 0] = dk[FRAMES:].astype(BF16)
+            dkv1[p, 1] = dv[FRAMES:].astype(BF16)
+            db = db.reshape(NY, 2, 2, 16, LANES)
+            band[p] = db
+            band16[p] = db.astype(BF16)
+        for p in ps:
+            pltpu.make_async_copy(dqv.at[p], dq_ref.at[0, :, cols(p)], out_sem.at[0]).start()
 
     def send_back(k):
         part = chunk(k, REDUCE)
@@ -271,35 +297,42 @@
         for n, ref in ((0, dk_ref), (1, dv_ref)):
             pltpu.make_async_copy(dkvo.at[p, n], ref.at[0, :, cols(p)], out_sem.at[1]).start()
 
-    done = 0
-    share_table(0)
-    pass_on(3)
-    share_table(1)
-    along_y(4, sz)
-    pass_on(4)
-    shift(4)
-    for k, (start, number) in enumerate(GATHER):
+    done = summed = 0
+    for k in (0, 1):
+        gather_wait(k)
+        share_table(k)
+    hand_round()
+
+    def table_wait(k):
         wait_bytes(tab.at[chunk(k, GATHER), :, :, 0], c_r.at[k])
-        for p in range(start, start + number):
-            pair_step(p)
-            if p == start and k + 2 < chunks:
-                share_table(k + 2)
-            if p + 1 == sum(REDUCE[done]):
-                send_back(done)
-                if done >= 1:
-                    chip_sum(done - 1)
-                done += 1
+
+    for ps in TOGETHER:
+        for k, (start, _) in enumerate(GATHER):
+            if start in ps:
+                table_wait(k)
+        pair_steps(*ps)
+        if 0 in ps:
+            gather_wait(2)
+            share_table(2)
+        if 2 in ps:
+            wait_bytes(tab.at[pl.ds(0, NX - 1), :, :, 0], h_r)
+            for later in range(SPLIT, chunks):
+                share_table(later)
+        while done < len(REDUCE) and sum(REDUCE[done]) - 1 <= ps[-1]:
+            send_back(done)
+            done += 1
+        while summed < done - LAG:
+            chip_sum(summed)
+            summed += 1
     last = len(REDUCE) - 1
     y_sum(0)
-    chip_sum(last)
-    y_sum(1)
-    x_sum(0)
-    y_sum(2)
-    y_sum(3)
-    x_sum(1)
-    y_sum(last)
-    x_sum(2)
-    x_sum(3)
+    for k in range(summed, last + 1):
+        chip_sum(k)
+    for k in range(1, last + 1):
+        y_sum(k)
+        if k >= 2:
+            x_sum(k - 2)
+    x_sum(last - 1)
     for p in range(pairs - 2):
         finish_keys(p)
     x_sum(last)
@@ -314,8 +347,10 @@
             dp_ref[15 - r : 16 - r, p * LANES : (p + 1) * LANES] = total[r : r + 1]
 
     wait_bytes(kvp, kv_s)
-    wait_bytes(tab.at[:, 0, 0, 0], z_s)
-    wait_bytes(tab.at[:, pl.ds(0, NY - 1), :, 0], y_s)
+    sent = pl.ds(0, GATHER[SPLIT][0] + 1)
+    wait_bytes(tab.at[sent, 0, 0, 0], z_s)
+    wait_bytes(tab.at[sent, pl.ds(0, NY - 1), :, 0], y_s)
+    wait_bytes(tab.at[pl.ds(0, NX - 1), :, :, 0], h_s)
     wait_bytes(tab.at[:, :, :, 0], c_s)
     wait_bytes(dkv1, b_s)
     wait_bytes(corer, bc_s)
@@ -373,6 +408,7 @@
         sem, sem((pairs,)),
         sem, gather,
         sem, gather,
+        sem, sem,
         sem, gather,
         sem, sem((pairs,)),
         sem, reduce,

time: 62 us -> 60.4 us (0.974)
  Pallas kernels: 61.2 us -> 59.6 us
    pallas_call x1, Pallas kernels: 59.3 us -> 57.7 us  [local(): pl.pallas_call(functools.partial(kernel, pairs), out_shape=results, in_sp...]
where the time goes in v4:
time: 60.4 us; the launch traced here: 60.2 us
  Pallas kernels  59.6 us (99%)
  between operations  0.64 us (1%)
    pallas_call x1, Pallas kernels, local(): pl.pallas_call(functools.partial(kernel, pairs), out_shape=results, in_sp...  57.7 us
    pallas_call x1, Pallas kernels, local(): pl.pallas_call(write_out, out_shape=results, in_specs=[hbm] * 4, out_spec...  1.91 us

profile of v4, /device:TPU:8, one launch (start us, length us, event | category | flops | bytes accessed | tf_op | source)
XLA Modules:
  0.0 60.2 jit_solution(6299171763977698124)
XLA Ops:
  0.6 57.7 %shard_map.102 = (bf16[1,128,1024]{2,1,0:T(8,128)(2,1)}, bf16[1,128,1024]{2,1,0:T(8,128)(2,1)}, bf16[1,128,1024]{2,1,0:T(8,128)(2,1)}, f32[16,1024]{1,0:T(8,128)}) custom-call(bf16[1,128,1024]{2,1,0:T(8,128)(2,1)} %q_ref.1, bf16[1,128,1024]{2,1,0:T(8,128)(2,1)} %k_ref.1, bf16[1,128,1024]{2,1,0:T(8,128)(2,1)} %v_ref.1, bf16[1,128,1024]{2,1,0:T(8,128)(2,1)} %g_ref.1, ...), custom_call_target="tpu_custom_call" | custom-call | tf_op jit(solution)/shard_map/pallas_call | solution.py:422
  58.3 1.9 %shard_map.103 = (bf16[1,128,1024]{2,1,0:T(8,128)(2,1)}, bf16[1,128,1024]{2,1,0:T(8,128)(2,1)}, bf16[1,128,1024]{2,1,0:T(8,128)(2,1)}, f32[16,1024]{1,0:T(8,128)}) custom-call(bf16[1,128,1024]{2,1,0:T(8,128)(2,1)} %get-tuple-element.8.refs_0_, bf16[1,128,1024]{2,1,0:T(8,128)(2,1)} %get-tuple-element.9.refs_1_, ...), custom_call_target="tpu_custom_call" | custom-call | tf_op jit(solution)/shard_map/pallas_call | solution.py:435

commit v5 on v4

--- a/solution.py
+++ b/solution.py
@@ -18,7 +18,7 @@
 SPLIT = 3
 LAG = 1
 TOGETHER = ((0,), (1,), (2,), (3,), (4, 5), (6,), (7,))
-REDUCE = ((0, 2), (2, 1), (3, 1), (4, 1), (5, 1), (6, 1), (7, 1))
+REDUCE = ((0, 1), (1, 1), (2, 1), (3, 1), (4, 1), (5, 1), (6, 1), (7, 1))
 
 
 def contract_lanes(a, b):
@@ -143,12 +143,12 @@
     def chunk(k, chunks):
         return pl.ds(*chunks[k])
 
+    pos_copy = pltpu.make_async_copy(pos_ref, posv, first_sem.at[0])
+    pos_copy.start()
     barrier = pltpu.get_barrier_semaphore()
     peers = [following, before] + y_peers + x_peers + z_peers
     for peer in peers:
         pl.semaphore_signal(barrier, inc=1, device_id=peer, device_id_type=MESH)
-    pos_copy = pltpu.make_async_copy(pos_ref, posv, first_sem.at[0])
-    pos_copy.start()
     bias_copies = [
         pltpu.make_async_copy(ref, biases.at[n], first_sem.at[1 + n]) for n, ref in enumerate((bc_ref, bp_ref))
     ]

time: 60.4 us -> 59.5 us (0.985)
  Pallas kernels: 59.6 us -> 58.7 us
    pallas_call x1, Pallas kernels: 57.7 us -> 56.8 us  [local(): pl.pallas_call(functools.partial(kernel, pairs), out_shape=results, in_sp...]
where the time goes in v5:
time: 59.5 us; the launch traced here: 59.3 us
  Pallas kernels  58.7 us (99%)
  between operations  0.64 us (1%)
    pallas_call x1, Pallas kernels, local(): pl.pallas_call(functools.partial(kernel, pairs), out_shape=results, in_sp...  56.8 us
    pallas_call x1, Pallas kernels, local(): pl.pallas_call(write_out, out_shape=results, in_specs=[hbm] * 4, out_spec...  1.91 us

profile of v5, /device:TPU:8, one launch (start us, length us, event | category | flops | bytes accessed | tf_op | source)
XLA Modules:
  0.0 59.3 jit_solution(9352249623705820700)
XLA Ops:
  0.6 56.8 %shard_map.102 = (bf16[1,128,1024]{2,1,0:T(8,128)(2,1)}, bf16[1,128,1024]{2,1,0:T(8,128)(2,1)}, bf16[1,128,1024]{2,1,0:T(8,128)(2,1)}, f32[16,1024]{1,0:T(8,128)}) custom-call(bf16[1,128,1024]{2,1,0:T(8,128)(2,1)} %q_ref.1, bf16[1,128,1024]{2,1,0:T(8,128)(2,1)} %k_ref.1, bf16[1,128,1024]{2,1,0:T(8,128)(2,1)} %v_ref.1, bf16[1,128,1024]{2,1,0:T(8,128)(2,1)} %g_ref.1, ...), custom_call_target="tpu_custom_call" | custom-call | tf_op jit(solution)/shard_map/pallas_call | solution.py:422
  57.4 1.9 %shard_map.103 = (bf16[1,128,1024]{2,1,0:T(8,128)(2,1)}, bf16[1,128,1024]{2,1,0:T(8,128)(2,1)}, bf16[1,128,1024]{2,1,0:T(8,128)(2,1)}, f32[16,1024]{1,0:T(8,128)}) custom-call(bf16[1,128,1024]{2,1,0:T(8,128)(2,1)} %get-tuple-element.8.refs_0_, bf16[1,128,1024]{2,1,0:T(8,128)(2,1)} %get-tuple-element.9.refs_1_, ...), custom_call_target="tpu_custom_call" | custom-call | tf_op jit(solution)/shard_map/pallas_call | solution.py:435
